TPU v7x, 256 devices: a whole 4x4x8 slice. The times are simulated.
256 devices in a mesh: group: 32 (over x, y, core), mp: 8 (over z).
Axes of the slice: x: 4, y: 4, z: 8, core: 2. Of those that a mesh axis runs over, the one named last changes fastest.
Arguments:
- hidden: bfloat16 [16384, 1792], P('group')
- norm_gain: float32 [1792], replicated, may hold values from 0.1 to 1.9
- qkv_weight: bfloat16 [1792, 2304], P(None, 'mp'), may hold values from -0.125 to 0.125
- out_weight: bfloat16 [1792, 1792], P('mp'), may hold values from -0.125 to 0.125
- adapter_down: bfloat16 [1792, 1024], P(None, 'mp'), may hold values from -0.125 to 0.125
- adapter_up: bfloat16 [1024, 1792], P('mp'), may hold values from -1.5 to 1.5
- vocab_rows: bfloat16 [4096, 1792], P(('group', 'mp')), may hold values from -0.125 to 0.125
- segments: int32 [16384], P('group'), may hold values from 0 to 127, never falling along the last dimension, each value on 1 to 512 neighbouring positions
- request_adapter: int32 [128], replicated, may hold values from 0 to 63
- adapter_slot: int32 [64], replicated, may hold values from 0 to 63, each once
- page_table: int32 [2048], replicated, may hold values from 0 to 2047, as said below
Outputs:
- layer_update: bfloat16 [16384, 1792], P('group', 'mp')
- state_norms: float32 [16, 16384], P('mp', 'group')
- max_logits: float32 [16384], P(('group', 'mp'))
Inputs may be any that keep to these rules, and one draw needn't show every extreme that they name: A permutation of all pages. Logical page k of group g (entry g * 64 + k) lies in group page_table[g * 64 + k] // 64, and every group holds exactly two of the logical pages of every group. `segments`: every request's tokens stand together and in order; no request has more than 512 tokens. `adapter_slot`: A permutation.
All inputs are finite; a program needn't handle non-finite values.
Results may differ from a plain program's by a relative error of at most 0.013.
Values may be sent and summed in bfloat16 or wider, within the bound.
A program may use at most 64 MiB of HBM per device.

v0:
```python
import jax
import jax.numpy as jnp
from jax import lax
from jax.sharding import PartitionSpec as P

FEAT = 16
HD = 112
RANK = 16
EPSILON = 1e-05
PRECISE = lax.Precision.HIGHEST


def from_behind(value, axis, by):
    size = lax.axis_size(axis)
    pairs = [(i, i + by) for i in range(size) if 0 <= i + by < size]
    return lax.ppermute(value, axis, pairs)


def rms_normed(values, norm_gain):
    wide = values.astype(jnp.float32)
    meansq = jnp.mean(wide * wide, axis=-1, keepdims=True)
    return (wide * lax.rsqrt(meansq + EPSILON) * norm_gain).astype(jnp.bfloat16)


def features(vectors, feat_width):
    linear_part = vectors / feat_width**0.25
    outer_part = (vectors[..., :, None] * vectors[..., None, :]).reshape(
        vectors.shape[:-1] + (feat_width * feat_width,)
    )
    outer_part = outer_part / (2.0 * feat_width) ** 0.5
    ones_part = jnp.ones(vectors.shape[:-1] + (1,), jnp.float32)
    return jnp.concatenate([ones_part, linear_part, outer_part], axis=-1)


def block_step(state_carry, block_inputs, feat_width):
    states, totals, owner_seg = state_carry
    phi_query, phi_key, query_rows, key_rows, value_rows, seg_ids = block_inputs
    scaling = feat_width ** (-0.5)
    block_len = seg_ids.shape[0]
    position = jnp.arange(block_len, dtype=jnp.int32)
    allowed = (
        (position[:, None] >= position[None, :]) & (seg_ids[:, None] == seg_ids[None, :])
    ).astype(jnp.float32)
    carried = (seg_ids == owner_seg).astype(jnp.float32)[None, :]
    scores = jnp.einsum("hcf,hdf->hcd", query_rows, key_rows, precision=PRECISE) * scaling
    weights = (1.0 + scores + 0.5 * scores * scores) * allowed[None]
    numerator = jnp.einsum("hcd,hde->hce", weights, value_rows, precision=PRECISE)
    numerator = numerator + carried[..., None] * jnp.einsum(
        "hcp,hpe->hce", phi_query, states, precision=PRECISE
    )
    denominator = jnp.sum(weights, axis=-1) + carried * jnp.einsum(
        "hcp,hp->hc", phi_query, totals, precision=PRECISE
    )
    mixed_out = numerator / denominator[..., None]
    key_scores = jnp.einsum("hcf,hdf->hcd", key_rows, key_rows, precision=PRECISE) * scaling
    value_gram = jnp.einsum("hce,hde->hcd", value_rows, value_rows, precision=PRECISE)
    key_gram = (1.0 + key_scores + 0.5 * key_scores * key_scores) * value_gram
    masked_gram = jnp.einsum("cd,hde->hce", allowed, key_gram, precision=PRECISE)
    local_squares = jnp.sum(masked_gram * allowed[None], axis=-1)
    along = jnp.sum(
        jnp.einsum("hcp,hpe->hce", phi_key, states, precision=PRECISE) * value_rows, axis=-1
    )
    cross_squares = jnp.einsum("cd,hd->hc", allowed, along, precision=PRECISE)
    state_squares = jnp.sum(states * states, axis=(1, 2))
    squares = carried * (state_squares[:, None] + 2.0 * cross_squares) + local_squares
    counted = carried * totals[:, :1] + jnp.sum(allowed, axis=-1)[None, :]
    state_norm = jnp.sqrt(squares / (counted * (feat_width * value_rows.shape[-1])))
    last_seg = seg_ids[-1]
    member = (seg_ids == last_seg).astype(jnp.float32)
    continues = (owner_seg == last_seg).astype(jnp.float32)
    new_states = continues * states + jnp.einsum(
        "hcp,hce->hpe", phi_key * member[None, :, None], value_rows, precision=PRECISE
    )
    new_totals = continues * totals + jnp.einsum("hcp,c->hp", phi_key, member, precision=PRECISE)
    return ((new_states, new_totals, last_seg), (mixed_out, state_norm))


def best_of(candidates, piece):
    logits = jnp.einsum("rd,vd->rv", candidates, piece, preferred_element_type=jnp.float32)
    return jnp.max(logits, axis=1)


def on_device(
    hidden,
    norm_gain,
    qkv_weight,
    out_weight,
    adapter_down,
    adapter_up,
    vocab_rows,
    segments,
    request_adapter,
    adapter_slot,
    page_table,
):
    groups = lax.axis_size("group")
    own_group = lax.axis_index("group")
    shards = lax.axis_size("mp")
    own_shard = lax.axis_index("mp")
    rows_here = segments.shape[0]
    model_width = hidden.shape[1]
    slice_width = model_width // shards
    table = page_table.reshape(groups, -1)
    per_group = table.shape[1]
    per_peer = per_group // groups
    page_len = rows_here // per_group
    holders = table // per_group
    position = jnp.arange(per_group, dtype=jnp.int32)
    sort_keys = jnp.where(holders == own_group, position[None, :], per_group + position[None, :])
    ranked = jnp.argsort(sort_keys, axis=1)[:, :per_peer]
    picked = jnp.take_along_axis(table, ranked, axis=1) - own_group * per_group
    outgoing = hidden.reshape(per_group, page_len, model_width)[picked]
    normed_pages = rms_normed(outgoing, norm_gain)
    projected_pages = jnp.einsum(
        "abrd,dc->abrc", normed_pages, qkv_weight, preferred_element_type=jnp.float32
    ).astype(jnp.bfloat16)
    lowered_pages = jnp.einsum(
        "abrd,dc->abrc", normed_pages, adapter_down, preferred_element_type=jnp.float32
    ).astype(jnp.bfloat16)
    kept_pages = lax.dynamic_slice_in_dim(outgoing, own_shard * slice_width, slice_width, 3)
    arrived = (
        lax.all_to_all(kept_pages, "group", split_axis=0, concat_axis=0, tiled=True),
        lax.all_to_all(projected_pages, "group", split_axis=0, concat_axis=0, tiled=True),
        lax.all_to_all(lowered_pages, "group", split_axis=0, concat_axis=0, tiled=True),
    )
    own_holders = lax.dynamic_index_in_dim(holders, own_group, 0, keepdims=False)
    onehot = (own_holders[:, None] == jnp.arange(groups, dtype=jnp.int32)[None, :]).astype(
        jnp.int32
    )
    earlier = jnp.sum((jnp.cumsum(onehot, axis=0) - onehot) * onehot, axis=1)
    source_rows = own_holders * per_peer + earlier

    def placed(received):
        gathered_rows = received.reshape((groups * per_peer,) + received.shape[2:])[source_rows]
        return gathered_rows.reshape((rows_here,) + received.shape[3:])

    residual, projected, lowered = [placed(received) for received in arrived]
    group_vocab = lax.all_gather(vocab_rows, "group", axis=0, tiled=True)
    group_vocab, projected = lax.optimization_barrier((group_vocab, projected))
    heads_here = projected.shape[1] // (2 * FEAT + HD)
    split_heads = jnp.transpose(
        projected.reshape(rows_here, heads_here, 2 * FEAT + HD).astype(jnp.float32), (1, 0, 2)
    )
    query_rows = split_heads[..., :FEAT]
    key_rows = split_heads[..., FEAT : 2 * FEAT]
    value_rows = split_heads[..., 2 * FEAT :]
    phi_query = features(query_rows, FEAT)
    phi_key = features(key_rows, FEAT)
    last_seg = segments[-1]
    member = (segments == last_seg).astype(jnp.float32)
    end_state = jnp.einsum(
        "hcp,hce->hpe", phi_key * member[None, :, None], value_rows, precision=PRECISE
    )
    end_totals = jnp.einsum("hcp,c->hp", phi_key, member, precision=PRECISE)
    end_tag = jnp.reshape(last_seg + 1, (1,)).astype(jnp.float32)
    got_state, got_totals, got_tag = (
        from_behind(end_state.astype(jnp.bfloat16), "group", 1).astype(end_state.dtype),
        from_behind(end_totals.astype(jnp.bfloat16), "group", 1).astype(end_totals.dtype),
        from_behind(end_tag.astype(jnp.bfloat16), "group", 1).astype(end_tag.dtype),
    )
    initial = (got_state, got_totals, got_tag[0].astype(jnp.int32) - 1)
    block_len = min(256, rows_here)
    blocks = rows_here // block_len

    def regroup(values):
        return jnp.transpose(
            values.reshape(values.shape[0], blocks, block_len, values.shape[-1]), (1, 0, 2, 3)
        )

    scan_inputs = (
        regroup(phi_query),
        regroup(phi_key),
        regroup(query_rows),
        regroup(key_rows),
        regroup(value_rows),
        segments.reshape(blocks, block_len),
    )

    def scan_step(state_carry, block_inputs):
        return block_step(state_carry, block_inputs, FEAT)

    _, (mixed_out, state_norm) = lax.scan(scan_step, initial, scan_inputs)
    attended = (
        jnp.transpose(mixed_out, (0, 2, 1, 3))
        .reshape(rows_here, heads_here * HD)
        .astype(jnp.bfloat16)
    )
    state_norms = jnp.transpose(state_norm, (1, 0, 2)).reshape(heads_here, rows_here)
    request_ids = jnp.arange(request_adapter.shape[0], dtype=jnp.int32)
    adapter_of = jnp.sum(
        jnp.where(segments[:, None] == request_ids[None, :], request_adapter[None, :], 0), axis=1
    )
    adapter_ids = jnp.arange(adapter_slot.shape[0], dtype=jnp.int32)
    slot_ids = jnp.sum(
        jnp.where(adapter_of[:, None] == adapter_ids[None, :], adapter_slot[None, :], 0), axis=1
    )
    column_slot = jnp.arange(lowered.shape[1], dtype=jnp.int32) // RANK
    local_slot = slot_ids - own_shard * (lowered.shape[1] // RANK)
    low_rank = jnp.where(
        local_slot[:, None] == column_slot[None, :], lowered, jnp.zeros_like(lowered)
    )
    partial_value = jnp.dot(attended, out_weight, preferred_element_type=jnp.float32)
    partial_value = partial_value + jnp.dot(
        low_rank, adapter_up, preferred_element_type=jnp.float32
    )
    summed = lax.psum_scatter(
        partial_value.astype(jnp.bfloat16), "mp", scatter_dimension=1, tiled=True
    )
    final_rows = (residual.astype(jnp.float32) + summed.astype(jnp.float32)).astype(jnp.bfloat16)
    group_rows = lax.all_gather(final_rows, "mp", axis=1, tiled=True)
    partial_best = best_of(group_rows, group_vocab)
    max_logits = lax.dynamic_slice_in_dim(
        lax.pmax(partial_best, "mp"), own_shard * (rows_here // shards), rows_here // shards
    )
    return (summed, state_norms, max_logits)


def solution(mesh):
    placed = (
        P("group", None),
        P(),
        P(None, "mp"),
        P("mp", None),
        P(None, "mp"),
        P("mp", None),
        P(("group", "mp"), None),
        P("group"),
        P(),
        P(),
        P(),
    )
    return jax.shard_map(
        on_device,
        mesh=mesh,
        in_specs=placed,
        out_specs=(P("group", "mp"), P("mp", "group"), P(("group", "mp"))),
        check_vma=False,
    )
```

profile of v0, /device:TPU:2, one launch (start us, length us, event | category | flops | bytes accessed | tf_op | source)
XLA Modules:
  0.0 222.2 jit_solution(6068181078464134090)
XLA Ops:
  9.8 2.7 %collective-permute-start.2 = (bf16[1]{0:T(256)(128)(2,1)}, bf16[1]{0:T(256)(128)(2,1)}, u32[]{:S(2)}, u32[]{:S(2)}) collective-permute-start(bf16[1]{0:T(256)(128)(2,1)} %bitcast.33), channel_id=1, source_target_pairs={{0,8},{8,16},{16,24},{24,32},{32,40},{40,48},{48,56},{56,64},{64,7... | collective-permute-start | bytes 14 | tf_op jit(solution)/shard_map/ppermute | solution.py:16
  15.9 1.9 gather_fusion
  17.8 2.0 fusion.49
  20.0 3.0 %fusion.59 = bf16[32,2,8,128]{3,2,1,0:T(8,128)(2,1)} fusion(bf16[32,2,8,1792]{3,2,1,0:T(8,128)(2,1)} %bitcast.226, f32[1792]{0:T(1024)S(1)} %copy-done.14, f32[32,2,8]{2,1,0:T(2,128)S(1)} %copy.89, bf16[1792,128]{1,0:T(8,128)(2,1)} %param.17), kind=kOutput, calls=%fused_computation.84 | convolution fusion | flops 238616576 | bytes 2434048 | tf_op jit(solution)/shard_map/abrd,dc->abrc/dot_general | solution.py:117
  23.0 8.5 %all-to-all-start.1 = ((bf16[32,2,8,128]{3,2,1,0:T(8,128)(2,1)}), bf16[32,2,8,128]{3,2,1,0:T(8,128)(2,1)S(1)}, u32[]{:S(2)}, u32[]{:S(2)}) async-start(bf16[32,2,8,128]{3,2,1,0:T(8,128)(2,1)} %fusion.59), calls=%async_computation.1 | async-start | bytes 262144 | tf_op jit(solution)/shard_map/all_to_all | solution.py:124
  32.8 3.4 %fusion.56 = bf16[32,2,8,288]{3,2,1,0:T(8,128)(2,1)} fusion(bf16[32,2,8,1792]{3,2,1,0:T(8,128)(2,1)} %bitcast.227, f32[1792]{0:T(1024)S(1)} %copy-done.14, f32[32,2,8]{2,1,0:T(2,128)S(1)} %copy.89, bf16[1792,288]{0,1:T(8,128)(2,1)S(1)} %copy-done.13), kind=kOutput, calls=%fused_computation.81 | convolution fusion | flops 532299776 | bytes 3171328 | tf_op jit(solution)/shard_map/abrd,dc->abrc/dot_general | solution.py:114
  36.4 1.8 all-to-all-done.1
  38.2 5.6 %all-to-all-start = ((bf16[32,2,8,288]{3,2,1,0:T(8,128)(2,1)}), bf16[32,2,8,288]{3,2,1,0:T(8,128)(2,1)S(1)}, u32[]{:S(2)}, u32[]{:S(2)}) async-start(bf16[32,2,8,288]{3,2,1,0:T(8,128)(2,1)} %fusion.56), calls=%async_computation | async-start | bytes 786432 | tf_op jit(solution)/shard_map/all_to_all | solution.py:123
  46.4 6.2 %all-to-all-done = bf16[32,2,8,288]{3,2,1,0:T(8,128)(2,1)S(1)} async-done(((bf16[32,2,8,288]{3,2,1,0:T(8,128)(2,1)}), bf16[32,2,8,288]{3,2,1,0:T(8,128)(2,1)S(1)}, u32[]{:S(2)}, u32[]{:S(2)}) %all-to-all-start) | async-done | bytes 294944 | tf_op jit(solution)/shard_map/all_to_all | solution.py:123
  53.2 9.2 %all-gather.3.cloned.1.call-done = bf16[512,1792]{1,0:T(8,128)(2,1)} async-done(((bf16[16,1792]{1,0:T(8,128)(2,1)}), bf16[512,1792]{1,0:T(8,128)(2,1)}) %all-gather.3.cloned.1.call-update) | async-done | bytes 1835024 | tf_op jit(solution)/shard_map/all_gather | solution.py:138
  64.3 1.3 convolution_convert_fusion
  66.5 2.2 collective-permute-start.1
  68.6 2.4 %collective-permute-start = (bf16[2,273,112]{2,1,0:T(8,128)(2,1)}, bf16[2,273,112]{2,1,0:T(8,128)(2,1)}, u32[]{:S(2)}, u32[]{:S(2)}) collective-permute-start(bf16[2,273,112]{2,1,0:T(8,128)(2,1)} %convolution_convert_fusion), channel_id=1, source_target_pairs={{0,8},{8,16},{16,24},{24,32},{32,40},{40,48},{48,56},{56,64},{64,7... | collective-permute-start | bytes 366920 | tf_op jit(solution)/shard_map/ppermute | solution.py:16
  72.5 1.7 reshape.246
  75.3 3.0 %reshape.250 = f32[2,2,256,273]{2,1,3,0:T(2,128)} reshape(f32[2,512,273]{1,2,0:T(8,128)} %get-tuple-element.279) | data formatting | bytes 2236416 | tf_op jit(solution)/shard_map/reshape | solution.py:167
  80.2 25.4 %while.21 = (s32[]{:T(128)}, f32[2,273,112]{2,1,0:T(8,128)S(1)}, f32[2,273]{0,1:T(8,128)S(1)}, s32[]{:T(128)}, bf16[2,2,256,112]{2,3,1,0:T(8,128)(2,1)}, /*index...) while((s32[]{:T(128)}, f32[2,273,112]{2,1,0:T(8,128)S(1)}, ...), condition=%wide.region_10.11_spmd, body=%wide.region_4.10_spmd.sunk | while | flops 1377437056 | bytes 23302216 | solution.py:182
  106.8 1.9 fusion.82
  108.7 2.0 add_convert_fusion
  111.9 15.2 %all_to_all.15 = bf16[32,2,8,224]{3,2,1,0:T(8,128)(2,1)S(1)} all-to-all(bf16[32,2,8,224]{3,2,1,0:T(8,128)(2,1)S(1)} %constant_dynamic-slice_fusion.3), channel_id=1, replica_groups=mesh['group'=32,'mp'=8] {'group'}, dimensions={0} | all-to-all | bytes 458752 | tf_op jit(solution)/shard_map/all_to_all | solution.py:122
  128.2 26.6 %reduce-scatter.2.cloned.1.call-done = bf16[512,224]{0,1:T(8,128)(2,1)} async-done(((bf16[512,1792]{0,1:T(8,128)(2,1)}), bf16[512,224]{0,1:T(8,128)(2,1)}) %reduce-scatter.2.cloned.1.call-update) | async-done | bytes 229392 | tf_op jit(solution)/shard_map/reduce_scatter | solution.py:206
  154.7 1.7 add_convert_fusion.1
  156.4 39.4 %all-gather.5.cloned.1.call-done = bf16[512,1792]{0,1:T(8,128)(2,1)} async-done(((bf16[512,224]{0,1:T(8,128)(2,1)}), bf16[512,1792]{0,1:T(8,128)(2,1)}) %all-gather.5.cloned.1.call-update) | async-done | bytes 1835024 | tf_op jit(solution)/shard_map/all_gather | solution.py:210
  195.8 3.2 %convolution_reduce_fusion = f32[512]{0:T(512)S(1)} fusion(bf16[512,1792]{1,0:T(8,128)(2,1)} %all-gather.3.cloned.1.call-done, bf16[512,1792]{0,1:T(8,128)(2,1)} %all-gather.5.cloned.1.call-done), kind=kOutput, calls=%fused_computation.82 | convolution fusion | flops 939785728 | bytes 3672064 | tf_op jit(solution)/shard_map/rd,vd->rv/dot_general | solution.py:79
  199.0 16.1 %pmax.7 = f32[512]{0:T(512)S(1)} all-reduce(f32[512]{0:T(512)S(1)} %convolution_reduce_fusion), channel_id=1, replica_groups=mesh['group'=32,'mp'=8] {'mp'}, use_global_device_ids=true, to_apply=%region_15.16 | all-reduce | flops 512 | bytes 4096 | tf_op jit(solution)/shard_map/pmax | solution.py:213
  (153 shorter events, 42.8 us)
Async XLA Ops:
  7.2 8.7 %copy-start = (bf16[512,1792]{1,0:T(8,128)(2,1)S(1)}, bf16[512,1792]{1,0:T(8,128)(2,1)}, u32[]{:S(2)}) copy-start(bf16[512,1792]{1,0:T(8,128)(2,1)} %param.13) | copy-start | bytes 5505028
  7.2 55.2 %all-gather.3.cloned.1.call-start = ((), (), s32[]{:S(2)}) async-start(), calls=%async_computation.4 | async-start | bytes 1892352 | tf_op jit(solution)/shard_map/all_gather | solution.py:138
  9.8 34.6 %collective-permute-start.2 = (bf16[1]{0:T(256)(128)(2,1)}, bf16[1]{0:T(256)(128)(2,1)}, u32[]{:S(2)}, u32[]{:S(2)}) collective-permute-start(bf16[1]{0:T(256)(128)(2,1)} %bitcast.33), channel_id=1, source_target_pairs={{0,8},{8,16},{16,24},{24,32},{32,40},{40,48},{48,56},{56,64},{64,7... | collective-permute-start | bytes 14 | tf_op jit(solution)/shard_map/ppermute | solution.py:16
  17.8 2.1 copy-start.14
  20.0 11.9 %copy-start.8 = (s32[512]{0:T(512)S(1)}, s32[512]{0:T(512)}, u32[]{:S(2)}) copy-start(s32[512]{0:T(512)} %param.20) | copy-start | bytes 6148
  20.0 11.9 %copy-start.11 = (s32[128]{0:T(128)S(1)}, s32[128]{0:T(128)}, u32[]{:S(2)}) copy-start(s32[128]{0:T(128)} %param.21) | copy-start | bytes 1540
  20.0 12.8 %copy-start.13 = (bf16[1792,288]{0,1:T(8,128)(2,1)S(1)}, bf16[1792,288]{0,1:T(8,128)(2,1)}, u32[]{:S(2)}) copy-start(bf16[1792,288]{0,1:T(8,128)(2,1)} %param.15) | copy-start | bytes 3096580
  23.0 15.2 %all-to-all-start.1 = ((bf16[32,2,8,128]{3,2,1,0:T(8,128)(2,1)}), bf16[32,2,8,128]{3,2,1,0:T(8,128)(2,1)S(1)}, u32[]{:S(2)}, u32[]{:S(2)}) async-start(bf16[32,2,8,128]{3,2,1,0:T(8,128)(2,1)} %fusion.59), calls=%async_computation.1 | async-start | bytes 262144 | tf_op jit(solution)/shard_map/all_to_all | solution.py:124
  32.8 3.5 %copy-start.12 = (s32[64]{0:T(128)S(1)}, s32[64]{0:T(128)}, u32[]{:S(2)}) copy-start(s32[64]{0:T(128)} %param.22) | copy-start | bytes 772
  36.3 26.4 %copy-start.9 = (s32[1024]{0:T(1024)}, s32[1024]{0:T(1024)S(1)}, u32[]{:S(2)}) copy-start(s32[1024]{0:T(1024)S(1)} %pad_clamp_fusion) | copy-start | bytes 12292
  38.2 14.3 %all-to-all-start = ((bf16[32,2,8,288]{3,2,1,0:T(8,128)(2,1)}), bf16[32,2,8,288]{3,2,1,0:T(8,128)(2,1)S(1)}, u32[]{:S(2)}, u32[]{:S(2)}) async-start(bf16[32,2,8,288]{3,2,1,0:T(8,128)(2,1)} %fusion.56), calls=%async_computation | async-start | bytes 786432 | tf_op jit(solution)/shard_map/all_to_all | solution.py:123
  43.8 110.9 %reduce-scatter.2.cloned.1.call-start = ((), (), s32[]{:S(2)}) async-start(), calls=%async_computation.5 | async-start | bytes 2064384 | tf_op jit(solution)/shard_map/reduce_scatter | solution.py:206
  66.5 11.8 %collective-permute-start.1 = (bf16[2,273]{0,1:T(8,128)(2,1)S(1)}, bf16[2,273]{0,1:T(8,128)(2,1)}, u32[]{:S(2)}, u32[]{:S(2)}) collective-permute-start(bf16[2,273]{0,1:T(8,128)(2,1)S(1)} %bitcast.252), channel_id=1, source_target_pairs={{0,8},{8,16},{16,24},{24,32},{32,40},{40,48},{48,56},{56,64},{64,7... | collective-permute-start | bytes 3284 | tf_op jit(solution)/shard_map/ppermute | solution.py:16
  68.6 10.6 %collective-permute-start = (bf16[2,273,112]{2,1,0:T(8,128)(2,1)}, bf16[2,273,112]{2,1,0:T(8,128)(2,1)}, u32[]{:S(2)}, u32[]{:S(2)}) collective-permute-start(bf16[2,273,112]{2,1,0:T(8,128)(2,1)} %convolution_convert_fusion), channel_id=1, source_target_pairs={{0,8},{8,16},{16,24},{24,32},{32,40},{40,48},{48,56},{56,64},{64,7... | collective-permute-start | bytes 366920 | tf_op jit(solution)/shard_map/ppermute | solution.py:16
  74.2 5.9 %copy-start.7 = (f32[2,2,256,16]{2,3,1,0:T(8,128)S(1)}, f32[2,2,256,16]{2,3,1,0:T(8,128)}, u32[]{:S(2)}) copy-start(f32[2,2,256,16]{2,3,1,0:T(8,128)} %get-tuple-element.383) | copy-start | bytes 196612
  82.8 2.6 %copy-start.1 = (f32[2,2,256,273]{2,0,3,1:T(2,128)S(1)}, f32[2,2,256,273]{2,0,3,1:T(2,128)}, u32[]{:S(2)}) copy-start(f32[2,2,256,273]{2,0,3,1:T(2,128)} %get-tuple-element.411) | copy-start | bytes 3354628 | tf_op jit(solution)/shard_map/while
  82.8 2.6 %copy-start.2 = (f32[2,2,256,273]{2,0,3,1:T(2,128)S(1)}, f32[2,2,256,273]{2,0,3,1:T(2,128)}, u32[]{:S(2)}) copy-start(f32[2,2,256,273]{2,0,3,1:T(2,128)} %get-tuple-element.415) | copy-start | bytes 3354628 | tf_op jit(solution)/shard_map/while
  85.4 2.5 %copy-start.5 = (bf16[2,2,256,112]{2,3,1,0:T(8,128)(2,1)S(1)}, bf16[2,2,256,112]{2,3,1,0:T(8,128)(2,1)}, u32[]{:S(2)}) copy-start(bf16[2,2,256,112]{2,3,1,0:T(8,128)(2,1)} %get-tuple-element.393) | copy-start | bytes 688132 | tf_op jit(solution)/shard_map/while
  88.4 3.8 %copy-start.6 = (bf16[2,2,256,112]{2,3,1,0:T(8,128)(2,1)}, bf16[2,2,256,112]{2,3,1,0:T(8,128)(2,1)S(1)}, u32[]{:S(2)}) copy-start(bf16[2,2,256,112]{2,3,1,0:T(8,128)(2,1)S(1)} %fusion.140) | copy-start | bytes 688132 | tf_op jit(solution)/shard_map/while
  95.4 2.6 %copy-start.1 = (f32[2,2,256,273]{2,0,3,1:T(2,128)S(1)}, f32[2,2,256,273]{2,0,3,1:T(2,128)}, u32[]{:S(2)}) copy-start(f32[2,2,256,273]{2,0,3,1:T(2,128)} %get-tuple-element.411) | copy-start | bytes 3354628 | tf_op jit(solution)/shard_map/while
  95.5 2.6 %copy-start.2 = (f32[2,2,256,273]{2,0,3,1:T(2,128)S(1)}, f32[2,2,256,273]{2,0,3,1:T(2,128)}, u32[]{:S(2)}) copy-start(f32[2,2,256,273]{2,0,3,1:T(2,128)} %get-tuple-element.415) | copy-start | bytes 3354628 | tf_op jit(solution)/shard_map/while
  98.0 2.5 %copy-start.5 = (bf16[2,2,256,112]{2,3,1,0:T(8,128)(2,1)S(1)}, bf16[2,2,256,112]{2,3,1,0:T(8,128)(2,1)}, u32[]{:S(2)}) copy-start(bf16[2,2,256,112]{2,3,1,0:T(8,128)(2,1)} %get-tuple-element.393) | copy-start | bytes 688132 | tf_op jit(solution)/shard_map/while
  101.0 3.8 %copy-start.6 = (bf16[2,2,256,112]{2,3,1,0:T(8,128)(2,1)}, bf16[2,2,256,112]{2,3,1,0:T(8,128)(2,1)S(1)}, u32[]{:S(2)}) copy-start(bf16[2,2,256,112]{2,3,1,0:T(8,128)(2,1)S(1)} %fusion.140) | copy-start | bytes 688132 | tf_op jit(solution)/shard_map/while
  110.7 85.1 %all-gather.5.cloned.1.call-start = ((), (), s32[]{:S(2)}) async-start(), calls=%async_computation.6 | async-start | bytes 2064384 | tf_op jit(solution)/shard_map/all_gather | solution.py:210
  (3 other events, 5.8 us)
Sparse Core Ops, SparseCore 0:
  10.6 51.8 all-gather.2
  110.9 43.7 reduce-scatter.1
  156.5 39.2 all-gather.4
where the time goes:
time: 223 us; the launch traced here: 222 us
  waiting for transfers between devices  83.9 us (38%)
  matrix products  31.4 us (14%)
  blocking collectives  31.4 us (14%)
  local copies, waits for them, and re-layouts  23.3 us (10%)
  starting transfers between devices  21.5 us (10%)
  between operations  15.5 us (7%)
  other arithmetic  12.4 us (6%)
  loops' own time  2.93 us (1%)
    all_gather x1, waiting for transfers between devices, on_device(): group_rows = lax.all_gather(final_rows, 'mp', axis=1, tiled=True)  39.4 us
    reduce_scatter x1, waiting for transfers between devices, on_device(): lax.psum_scatter(partial_value.astype(jnp.bfloat16), 'mp', scatter_dimens...  26.6 us
    pmax x1, blocking collectives, on_device(): lax.pmax(partial_best, 'mp')  16.1 us
    all_to_all x1, blocking collectives, on_device(): lax.all_to_all(kept_pages, 'group', split_axis=0, concat_axis=0, tiled=True)  15.2 us
    all_gather x1, waiting for transfers between devices, on_device(): group_vocab = lax.all_gather(vocab_rows, 'group', axis=0, tiled=True)  9.2 us
    all_to_all x1, starting transfers between devices, on_device(): lax.all_to_all(lowered_pages, 'group', split_axis=0, concat_axis=0, tiled...  8.52 us
    ppermute x3, starting transfers between devices, from_behind(): return lax.ppermute(value, axis, pairs)  7.28 us
    all_to_all x1, waiting for transfers between devices, on_device(): lax.all_to_all(projected_pages, 'group', split_axis=0, concat_axis=0, til...  6.21 us
  transfers between devices with their start and end apart: 8, of which 5 were waited for; matrix products, arithmetic and copies ran while one was open for 13% of the time, Pallas kernels for 0%

commit v1 on v0

--- a/solution.py
+++ b/solution.py
@@ -8,6 +8,14 @@
 RANK = 16
 EPSILON = 1e-05
 PRECISE = lax.Precision.HIGHEST
+
+
+def tiled_gather(shard, axis, dim):
+    devices = lax.axis_size(axis)
+    repeats = [devices if d == dim else 1 for d in range(shard.ndim)]
+    return lax.all_to_all(
+        jnp.tile(shard, repeats), axis, split_axis=dim, concat_axis=dim, tiled=True
+    )
 
 
 def from_behind(value, axis, by):
@@ -207,7 +215,7 @@
         partial_value.astype(jnp.bfloat16), "mp", scatter_dimension=1, tiled=True
     )
     final_rows = (residual.astype(jnp.float32) + summed.astype(jnp.float32)).astype(jnp.bfloat16)
-    group_rows = lax.all_gather(final_rows, "mp", axis=1, tiled=True)
+    group_rows = tiled_gather(final_rows, "mp", 1)
     partial_best = best_of(group_rows, group_vocab)
     max_logits = lax.dynamic_slice_in_dim(
         lax.pmax(partial_best, "mp"), own_shard * (rows_here // shards), rows_here // shards

time: 223 us -> 229 us (1.027)
  starting transfers between devices: 21.5 us -> 25.9 us
  waiting for transfers between devices: 83.9 us -> 87.9 us
    all_to_all x0 -> x1, waiting for transfers between devices: none -> 42.7 us  [tiled_gather(): lax.all_to_all(jnp.tile(shard, repeats), axis, split_axis=dim, concat_axi...]
    all_gather x1 -> x0, waiting for transfers between devices: 39.4 us -> none  [on_device(): group_rows = lax.all_gather(final_rows, 'mp', axis=1, tiled=True)]
    all_to_all x0 -> x1, starting transfers between devices: none -> 4.39 us  [tiled_gather(): lax.all_to_all(jnp.tile(shard, repeats), axis, split_axis=dim, concat_axi...]
  transfers between devices with their start and end apart: 8 -> 8, of which waited for: 5 -> 5; matrix products, arithmetic and copies ran while one was open for 13% -> 12% of each run, Pallas kernels for 0% -> 0%
where the time goes in v1:
time: 229 us; the launch traced here: 228 us
  waiting for transfers between devices  87.9 us (38%)
  matrix products  30.2 us (13%)
  blocking collectives  29.9 us (13%)
  starting transfers between devices  25.9 us (11%)
  local copies, waits for them, and re-layouts  24.1 us (11%)
  between operations  15.7 us (7%)
  other arithmetic  11.2 us (5%)
  loops' own time  2.99 us (1%)
    all_to_all x1, waiting for transfers between devices, tiled_gather(): lax.all_to_all(jnp.tile(shard, repeats), axis, split_axis=dim, concat_axi...  42.7 us
    reduce_scatter x1, waiting for transfers between devices, on_device(): lax.psum_scatter(partial_value.astype(jnp.bfloat16), 'mp', scatter_dimens...  26.7 us
    all_to_all x1, blocking collectives, on_device(): lax.all_to_all(kept_pages, 'group', split_axis=0, concat_axis=0, tiled=True)  15.2 us
    pmax x1, blocking collectives, on_device(): lax.pmax(partial_best, 'mp')  14.7 us
    all_gather x1, waiting for transfers between devices, on_device(): group_vocab = lax.all_gather(vocab_rows, 'group', axis=0, tiled=True)  9.2 us
    all_to_all x1, starting transfers between devices, on_device(): lax.all_to_all(lowered_pages, 'group', split_axis=0, concat_axis=0, tiled...  8.38 us
    ppermute x3, starting transfers between devices, from_behind(): return lax.ppermute(value, axis, pairs)  7.44 us
    all_to_all x1, waiting for transfers between devices, on_device(): lax.all_to_all(projected_pages, 'group', split_axis=0, concat_axis=0, til...  6.82 us
  transfers between devices with their start and end apart: 8, of which 5 were waited for; matrix products, arithmetic and copies ran while one was open for 12% of the time, Pallas kernels for 0%

profile of v1, /device:TPU:2, one launch (start us, length us, event | category | flops | bytes accessed | tf_op | source)
XLA Modules:
  0.0 228.0 jit_solution(18089982502119221653)
XLA Ops:
  9.8 2.9 %collective-permute-start.2 = (bf16[1]{0:T(256)(128)(2,1)}, bf16[1]{0:T(256)(128)(2,1)}, u32[]{:S(2)}, u32[]{:S(2)}) collective-permute-start(bf16[1]{0:T(256)(128)(2,1)} %bitcast.33), channel_id=1, source_target_pairs={{0,8},{8,16},{16,24},{24,32},{32,40},{40,48},{48,56},{56,64},{64,7... | collective-permute-start | bytes 14 | tf_op jit(solution)/shard_map/ppermute | solution.py:24
  16.0 1.9 gather_fusion
  17.9 2.0 fusion.49
  20.1 3.0 %fusion.59 = bf16[32,2,8,128]{3,2,1,0:T(8,128)(2,1)} fusion(bf16[32,2,8,1792]{3,2,1,0:T(8,128)(2,1)} %bitcast.227, f32[1792]{0:T(1024)S(1)} %copy-done.13, f32[32,2,8]{2,1,0:T(2,128)S(1)} %copy.90, bf16[1792,128]{1,0:T(8,128)(2,1)} %param.17), kind=kOutput, calls=%fused_computation.84 | convolution fusion | flops 238616576 | bytes 2434048 | tf_op jit(solution)/shard_map/abrd,dc->abrc/dot_general | solution.py:125
  23.1 8.4 %all-to-all-start.1 = ((bf16[32,2,8,128]{3,2,1,0:T(8,128)(2,1)}), bf16[32,2,8,128]{3,2,1,0:T(8,128)(2,1)S(1)}, u32[]{:S(2)}, u32[]{:S(2)}) async-start(bf16[32,2,8,128]{3,2,1,0:T(8,128)(2,1)} %fusion.59), calls=%async_computation.1 | async-start | bytes 262144 | tf_op jit(solution)/shard_map/all_to_all | solution.py:132
  32.8 3.4 %fusion.56 = bf16[32,2,8,288]{3,2,1,0:T(8,128)(2,1)} fusion(bf16[32,2,8,1792]{3,2,1,0:T(8,128)(2,1)} %bitcast.228, f32[1792]{0:T(1024)S(1)} %copy-done.13, f32[32,2,8]{2,1,0:T(2,128)S(1)} %copy.90, bf16[1792,288]{0,1:T(8,128)(2,1)S(1)} %copy-done.12), kind=kOutput, calls=%fused_computation.81 | convolution fusion | flops 532299776 | bytes 3171328 | tf_op jit(solution)/shard_map/abrd,dc->abrc/dot_general | solution.py:122
  36.4 1.8 all-to-all-done.1
  38.2 5.6 %all-to-all-start = ((bf16[32,2,8,288]{3,2,1,0:T(8,128)(2,1)}), bf16[32,2,8,288]{3,2,1,0:T(8,128)(2,1)S(1)}, u32[]{:S(2)}, u32[]{:S(2)}) async-start(bf16[32,2,8,288]{3,2,1,0:T(8,128)(2,1)} %fusion.56), calls=%async_computation | async-start | bytes 786432 | tf_op jit(solution)/shard_map/all_to_all | solution.py:131
  45.7 6.8 %all-to-all-done = bf16[32,2,8,288]{3,2,1,0:T(8,128)(2,1)S(1)} async-done(((bf16[32,2,8,288]{3,2,1,0:T(8,128)(2,1)}), bf16[32,2,8,288]{3,2,1,0:T(8,128)(2,1)S(1)}, u32[]{:S(2)}, u32[]{:S(2)}) %all-to-all-start) | async-done | bytes 294944 | tf_op jit(solution)/shard_map/all_to_all | solution.py:131
  53.2 9.2 %all-gather.2.cloned.1.call-done = bf16[512,1792]{1,0:T(8,128)(2,1)} async-done(((bf16[16,1792]{1,0:T(8,128)(2,1)}), bf16[512,1792]{1,0:T(8,128)(2,1)}) %all-gather.2.cloned.1.call-update) | async-done | bytes 1835024 | tf_op jit(solution)/shard_map/all_gather | solution.py:146
  67.1 2.2 collective-permute-start.1
  69.3 2.4 %collective-permute-start = (bf16[2,273,112]{2,1,0:T(8,128)(2,1)}, bf16[2,273,112]{2,1,0:T(8,128)(2,1)}, u32[]{:S(2)}, u32[]{:S(2)}) collective-permute-start(bf16[2,273,112]{2,1,0:T(8,128)(2,1)} %convolution_convert_fusion), channel_id=1, source_target_pairs={{0,8},{8,16},{16,24},{24,32},{32,40},{40,48},{48,56},{56,64},{64,7... | collective-permute-start | bytes 366920 | tf_op jit(solution)/shard_map/ppermute | solution.py:24
  73.2 1.7 reshape.253
  74.9 3.0 %reshape.257 = f32[2,2,256,273]{2,1,3,0:T(2,128)} reshape(f32[2,512,273]{1,2,0:T(8,128)} %get-tuple-element.279) | data formatting | bytes 2236416 | tf_op jit(solution)/shard_map/reshape | solution.py:175
  79.8 24.3 %while.21 = (s32[]{:T(128)}, f32[2,273,112]{2,1,0:T(8,128)S(1)}, f32[2,273]{0,1:T(8,128)S(1)}, s32[]{:T(128)}, bf16[2,2,256,112]{2,3,1,0:T(8,128)(2,1)}, /*index...) while((s32[]{:T(128)}, f32[2,273,112]{2,1,0:T(8,128)S(1)}, ...), condition=%wide.region_10.11_spmd, body=%wide.region_4.10_spmd.sunk | while | flops 1377437056 | bytes 23302216 | solution.py:190
  105.3 1.9 fusion.82
  107.2 2.0 add_convert_fusion
  110.4 15.2 %all_to_all.24 = bf16[32,2,8,224]{3,2,1,0:T(8,128)(2,1)S(1)} all-to-all(bf16[32,2,8,224]{3,2,1,0:T(8,128)(2,1)S(1)} %constant_dynamic-slice_fusion.3), channel_id=1, replica_groups=mesh['group'=32,'mp'=8] {'group'}, dimensions={0} | all-to-all | bytes 458752 | tf_op jit(solution)/shard_map/all_to_all | solution.py:130
  126.5 26.7 %reduce-scatter.2.cloned.1.call-done = bf16[512,224]{0,1:T(8,128)(2,1)} async-done(((bf16[512,1792]{0,1:T(8,128)(2,1)}), bf16[512,224]{0,1:T(8,128)(2,1)}) %reduce-scatter.2.cloned.1.call-update) | async-done | bytes 229392 | tf_op jit(solution)/shard_map/reduce_scatter | solution.py:214
  154.2 1.4 tile.2
  155.6 4.4 %all-to-all-start.3 = ((bf16[512,8,224]{0,2,1:T(8,128)(2,1)}), bf16[512,8,224]{0,2,1:T(8,128)(2,1)}, u32[]{:S(2)}, u32[]{:S(2)}) async-start(bf16[512,8,224]{0,2,1:T(8,128)(2,1)} %tile.2), calls=%async_computation.4 | async-start | bytes 3670016 | tf_op jit(solution)/shard_map/all_to_all | solution.py:16
  160.0 42.7 %all-to-all-done.3 = bf16[512,8,224]{0,2,1:T(8,128)(2,1)} async-done(((bf16[512,8,224]{0,2,1:T(8,128)(2,1)}), bf16[512,8,224]{0,2,1:T(8,128)(2,1)}, u32[]{:S(2)}, u32[]{:S(2)}) %all-to-all-start.3) | async-done | bytes 1835040 | tf_op jit(solution)/shard_map/all_to_all | solution.py:16
  202.7 3.2 %convolution_reduce_fusion = f32[512]{0:T(512)S(1)} fusion(bf16[512,1792]{1,0:T(8,128)(2,1)} %all-gather.2.cloned.1.call-done, bf16[512,1792]{0,1:T(8,128)(2,1)} %bitcast.50), kind=kOutput, calls=%fused_computation.82 | convolution fusion | flops 939785728 | bytes 3672064 | tf_op jit(solution)/shard_map/rd,vd->rv/dot_general | solution.py:87
  205.8 14.7 %pmax.7 = f32[512]{0:T(512)S(1)} all-reduce(f32[512]{0:T(512)S(1)} %convolution_reduce_fusion), channel_id=1, replica_groups=mesh['group'=32,'mp'=8] {'mp'}, use_global_device_ids=true, to_apply=%region_15.16 | all-reduce | flops 512 | bytes 4096 | tf_op jit(solution)/shard_map/pmax | solution.py:221
  (153 shorter events, 42.9 us)
Async XLA Ops:
  7.2 8.9 %copy-start = (bf16[512,1792]{1,0:T(8,128)(2,1)S(1)}, bf16[512,1792]{1,0:T(8,128)(2,1)}, u32[]{:S(2)}) copy-start(bf16[512,1792]{1,0:T(8,128)(2,1)} %param.13) | copy-start | bytes 5505028
  7.2 55.2 %all-gather.2.cloned.1.call-start = ((), (), s32[]{:S(2)}) async-start(), calls=%async_computation.5 | async-start | bytes 1892352 | tf_op jit(solution)/shard_map/all_gather | solution.py:146
  9.8 34.1 %collective-permute-start.2 = (bf16[1]{0:T(256)(128)(2,1)}, bf16[1]{0:T(256)(128)(2,1)}, u32[]{:S(2)}, u32[]{:S(2)}) collective-permute-start(bf16[1]{0:T(256)(128)(2,1)} %bitcast.33), channel_id=1, source_target_pairs={{0,8},{8,16},{16,24},{24,32},{32,40},{40,48},{48,56},{56,64},{64,7... | collective-permute-start | bytes 14 | tf_op jit(solution)/shard_map/ppermute | solution.py:24
  17.9 2.1 copy-start.13
  20.1 11.8 %copy-start.9 = (s32[512]{0:T(512)S(1)}, s32[512]{0:T(512)}, u32[]{:S(2)}) copy-start(s32[512]{0:T(512)} %param.20) | copy-start | bytes 6148
  20.1 11.8 %copy-start.10 = (s32[128]{0:T(128)S(1)}, s32[128]{0:T(128)}, u32[]{:S(2)}) copy-start(s32[128]{0:T(128)} %param.21) | copy-start | bytes 1540
  20.1 12.7 %copy-start.12 = (bf16[1792,288]{0,1:T(8,128)(2,1)S(1)}, bf16[1792,288]{0,1:T(8,128)(2,1)}, u32[]{:S(2)}) copy-start(bf16[1792,288]{0,1:T(8,128)(2,1)} %param.15) | copy-start | bytes 3096580
  23.1 15.1 %all-to-all-start.1 = ((bf16[32,2,8,128]{3,2,1,0:T(8,128)(2,1)}), bf16[32,2,8,128]{3,2,1,0:T(8,128)(2,1)S(1)}, u32[]{:S(2)}, u32[]{:S(2)}) async-start(bf16[32,2,8,128]{3,2,1,0:T(8,128)(2,1)} %fusion.59), calls=%async_computation.1 | async-start | bytes 262144 | tf_op jit(solution)/shard_map/all_to_all | solution.py:132
  32.8 3.5 %copy-start.11 = (s32[64]{0:T(128)S(1)}, s32[64]{0:T(128)}, u32[]{:S(2)}) copy-start(s32[64]{0:T(128)} %param.22) | copy-start | bytes 772
  38.2 14.3 %all-to-all-start = ((bf16[32,2,8,288]{3,2,1,0:T(8,128)(2,1)}), bf16[32,2,8,288]{3,2,1,0:T(8,128)(2,1)S(1)}, u32[]{:S(2)}, u32[]{:S(2)}) async-start(bf16[32,2,8,288]{3,2,1,0:T(8,128)(2,1)} %fusion.56), calls=%async_computation | async-start | bytes 786432 | tf_op jit(solution)/shard_map/all_to_all | solution.py:131
  43.8 109.4 %reduce-scatter.2.cloned.1.call-start = ((), (), s32[]{:S(2)}) async-start(), calls=%async_computation.6 | async-start | bytes 2064384 | tf_op jit(solution)/shard_map/reduce_scatter | solution.py:214
  67.1 10.8 %collective-permute-start.1 = (bf16[2,273]{0,1:T(8,128)(2,1)}, bf16[2,273]{0,1:T(8,128)(2,1)}, u32[]{:S(2)}, u32[]{:S(2)}) collective-permute-start(bf16[2,273]{0,1:T(8,128)(2,1)} %bitcast.141), channel_id=1, source_target_pairs={{0,8},{8,16},{16,24},{24,32},{32,40},{40,48},{48,56},{56,64},{64,7... | collective-permute-start | bytes 3284 | tf_op jit(solution)/shard_map/ppermute | solution.py:24
  69.3 9.6 %collective-permute-start = (bf16[2,273,112]{2,1,0:T(8,128)(2,1)}, bf16[2,273,112]{2,1,0:T(8,128)(2,1)}, u32[]{:S(2)}, u32[]{:S(2)}) collective-permute-start(bf16[2,273,112]{2,1,0:T(8,128)(2,1)} %convolution_convert_fusion), channel_id=1, source_target_pairs={{0,8},{8,16},{16,24},{24,32},{32,40},{40,48},{48,56},{56,64},{64,7... | collective-permute-start | bytes 366920 | tf_op jit(solution)/shard_map/ppermute | solution.py:24
  74.9 4.9 %copy-start.8 = (f32[2,2,256,16]{2,3,1,0:T(8,128)S(1)}, f32[2,2,256,16]{2,3,1,0:T(8,128)}, u32[]{:S(2)}) copy-start(f32[2,2,256,16]{2,3,1,0:T(8,128)} %get-tuple-element.383) | copy-start | bytes 196612
  82.4 2.6 %copy-start.1 = (f32[2,2,256,273]{2,0,3,1:T(2,128)S(1)}, f32[2,2,256,273]{2,0,3,1:T(2,128)}, u32[]{:S(2)}) copy-start(f32[2,2,256,273]{2,0,3,1:T(2,128)} %get-tuple-element.411) | copy-start | bytes 3354628 | tf_op jit(solution)/shard_map/while
  82.4 2.6 %copy-start.2 = (f32[2,2,256,273]{2,0,3,1:T(2,128)S(1)}, f32[2,2,256,273]{2,0,3,1:T(2,128)}, u32[]{:S(2)}) copy-start(f32[2,2,256,273]{2,0,3,1:T(2,128)} %get-tuple-element.415) | copy-start | bytes 3354628 | tf_op jit(solution)/shard_map/while
  85.0 2.5 %copy-start.6 = (bf16[2,2,256,112]{2,3,1,0:T(8,128)(2,1)S(1)}, bf16[2,2,256,112]{2,3,1,0:T(8,128)(2,1)}, u32[]{:S(2)}) copy-start(bf16[2,2,256,112]{2,3,1,0:T(8,128)(2,1)} %get-tuple-element.393) | copy-start | bytes 688132 | tf_op jit(solution)/shard_map/while
  88.0 3.3 %copy-start.7 = (bf16[2,2,256,112]{2,3,1,0:T(8,128)(2,1)}, bf16[2,2,256,112]{2,3,1,0:T(8,128)(2,1)S(1)}, u32[]{:S(2)}) copy-start(bf16[2,2,256,112]{2,3,1,0:T(8,128)(2,1)S(1)} %fusion.140) | copy-start | bytes 688132 | tf_op jit(solution)/shard_map/while
  94.5 2.6 %copy-start.1 = (f32[2,2,256,273]{2,0,3,1:T(2,128)S(1)}, f32[2,2,256,273]{2,0,3,1:T(2,128)}, u32[]{:S(2)}) copy-start(f32[2,2,256,273]{2,0,3,1:T(2,128)} %get-tuple-element.411) | copy-start | bytes 3354628 | tf_op jit(solution)/shard_map/while
  94.6 2.6 %copy-start.2 = (f32[2,2,256,273]{2,0,3,1:T(2,128)S(1)}, f32[2,2,256,273]{2,0,3,1:T(2,128)}, u32[]{:S(2)}) copy-start(f32[2,2,256,273]{2,0,3,1:T(2,128)} %get-tuple-element.415) | copy-start | bytes 3354628 | tf_op jit(solution)/shard_map/while
  97.1 2.5 %copy-start.6 = (bf16[2,2,256,112]{2,3,1,0:T(8,128)(2,1)S(1)}, bf16[2,2,256,112]{2,3,1,0:T(8,128)(2,1)}, u32[]{:S(2)}) copy-start(bf16[2,2,256,112]{2,3,1,0:T(8,128)(2,1)} %get-tuple-element.393) | copy-start | bytes 688132 | tf_op jit(solution)/shard_map/while
  100.1 3.3 %copy-start.7 = (bf16[2,2,256,112]{2,3,1,0:T(8,128)(2,1)}, bf16[2,2,256,112]{2,3,1,0:T(8,128)(2,1)S(1)}, u32[]{:S(2)}) copy-start(bf16[2,2,256,112]{2,3,1,0:T(8,128)(2,1)S(1)} %fusion.140) | copy-start | bytes 688132 | tf_op jit(solution)/shard_map/while
  104.1 3.2 %copy-start.14 = (f32[2,2,256]{2,1,0:T(2,128)}, f32[2,2,256]{2,1,0:T(2,128)S(1)}, u32[]{:S(2)}) copy-start(f32[2,2,256]{2,1,0:T(2,128)S(1)} %get-tuple-element.189) | copy-start | bytes 12292
  155.6 47.1 %all-to-all-start.3 = ((bf16[512,8,224]{0,2,1:T(8,128)(2,1)}), bf16[512,8,224]{0,2,1:T(8,128)(2,1)}, u32[]{:S(2)}, u32[]{:S(2)}) async-start(bf16[512,8,224]{0,2,1:T(8,128)(2,1)} %tile.2), calls=%async_computation.4 | async-start | bytes 3670016 | tf_op jit(solution)/shard_map/all_to_all | solution.py:16
  (3 other events, 5.6 us)
Sparse Core Ops, SparseCore 0:
  10.6 51.8 all-gather.1
  109.4 43.7 reduce-scatter.1
